TPU v7x, 256 devices: a whole 4x4x8 slice. The times are simulated.
256 devices in a mesh: sp: 64 (over y, z, core), dp: 4 (over x).
Axes of the slice: x: 4, y: 4, z: 8, core: 2. Of those that a mesh axis runs over, the one named last changes fastest.
Arguments:
- volume: bfloat16 [4, 96, 256, 8, 128], P('dp', None, 'sp'), may hold values from -6 to 6
- cotangent: bfloat16 [4, 96, 256, 8, 128], P('dp', None, 'sp'), may hold values from -6 to 6
- kernels_xy: bfloat16 [2, 96, 3, 3], replicated, may hold values from -2 to 2
- kernels_z: bfloat16 [2, 96, 3], replicated, may hold values from -3.5 to 3.5
- mixing: bfloat16 [2, 96, 96], replicated, may hold values from -0.625 to 0.625
Outputs:
- volume_grad: bfloat16 [4, 96, 256, 8, 128], P('dp', None, 'sp')
- mixing_grad: float32 [2, 96, 96], replicated
- xy_grad: float32 [2, 96, 3, 3], replicated
- z_grad: float32 [2, 96, 3], replicated
All inputs are finite; a program needn't handle non-finite values.
Results may differ from a plain program's by a relative error of at most 0.018.
Values may be sent and summed in bfloat16 or wider, within the bound.
A program may use at most 64 MiB of HBM per device.

v0:
```python
import math
import jax
import jax.numpy as jnp
from jax import lax
from jax.sharding import PartitionSpec as P


def padded_2(x, sides, width):
    for axis, dim in sides:
        count, length = (lax.axis_size(axis), x.shape[dim])
        up = [(i, (i + 1) % count) for i in range(count - 1)]
        down = [(j, i) for i, j in up]
        last = lax.slice_in_dim(x, length - width, length, axis=dim)
        first = lax.slice_in_dim(x, 0, width, axis=dim)
        before = lax.ppermute(last, axis, up)
        after = lax.ppermute(first, axis, down)
        x = jnp.concatenate([before, x, after], axis=dim)
    return x


def conv_plane(inputs, kernel):
    extent = inputs.shape[1] - 2
    across = inputs.shape[3]
    padded = jnp.pad(inputs, ((0, 0), (0, 0), (0, 0), (1, 1)))
    summed = jnp.zeros((inputs.shape[0], extent, inputs.shape[2], across), jnp.float32)
    for row_tap in range(3):
        for col_tap in range(3):
            summed = summed + kernel[:, row_tap, col_tap][:, None, None, None] * padded[
                :, row_tap : row_tap + extent, :, col_tap : col_tap + across
            ].astype(jnp.float32)
    return summed


def conv_depth(inputs, kernel):
    depth_len = inputs.shape[2]
    padded = jnp.pad(inputs, ((0, 0), (0, 0), (1, 1), (0, 0)))
    summed = jnp.zeros(inputs.shape, jnp.float32)
    for depth_tap in range(3):
        summed = (
            summed
            + kernel[:, depth_tap][:, None, None, None]
            * padded[:, :, depth_tap : depth_tap + depth_len, :]
        )
    return summed


def mix_channels(weights, inputs):
    channels = inputs.shape[0]
    flat = inputs.reshape(channels, -1)
    return jnp.dot(weights, flat, preferred_element_type=jnp.float32).reshape(inputs.shape)


def forward_block(inputs, kernel_xy, kernel_z, weights):
    planar = conv_plane(inputs, kernel_xy)
    axial = conv_depth(planar, kernel_z).astype(jnp.bfloat16)
    preact = mix_channels(weights, axial)
    return (planar, axial, preact)


def silu_slope(preact):
    sigma = jax.nn.sigmoid(preact)
    return sigma * (1.0 + preact * (1.0 - sigma))


def backward_block(grad_out, planar, axial, preact, around, kernel_z, weights, trim):
    grad_pre = (grad_out.astype(jnp.float32) * silu_slope(preact)).astype(jnp.bfloat16)
    channels = grad_pre.shape[0]
    grad_axial = jnp.dot(
        weights.T, grad_pre.reshape(channels, -1), preferred_element_type=jnp.float32
    ).reshape(grad_pre.shape)
    grad_planar = conv_depth(grad_axial, kernel_z[:, ::-1]).astype(jnp.bfloat16)
    extent = grad_pre.shape[1]
    own_extent = extent - 2 * trim
    own_pre = grad_pre.reshape(channels, -1)
    own_axial = axial.reshape(channels, -1)
    grad_weights = lax.dot_general(
        own_pre, own_axial, (((1,), (1,)), ((), ())), preferred_element_type=jnp.float32
    )
    depth_len = planar.shape[2]
    planar_pad = jnp.pad(planar, ((0, 0), (0, 0), (1, 1), (0, 0)))
    grad_kz = jnp.stack(
        [
            jnp.sum(
                grad_axial * planar_pad[:, :, depth_tap : depth_tap + depth_len, :], axis=(1, 2, 3)
            )
            for depth_tap in range(3)
        ],
        axis=1,
    )
    own_grad_planar = grad_planar.astype(jnp.float32)
    across = around.shape[3]
    around_pad = jnp.pad(around, ((0, 0), (0, 0), (0, 0), (1, 1)))
    rows_list = []
    for row_tap in range(3):
        cols_list = []
        for col_tap in range(3):
            cols_list.append(
                jnp.sum(
                    own_grad_planar
                    * around_pad[
                        :, row_tap : row_tap + own_extent, :, col_tap : col_tap + across
                    ].astype(jnp.float32),
                    axis=(1, 2, 3),
                )
            )
        rows_list.append(jnp.stack(cols_list, axis=1))
    grad_kxy = jnp.stack(rows_list, axis=1)
    return (grad_planar, (grad_weights, grad_kxy, grad_kz))


def edge_grads(grad_planar):
    return padded_2(grad_planar, (("sp", 1),), 1)


def settle_all(lower, upper):
    summed = lax.psum((lower[0], lower[1], lower[2], upper[0], upper[1], upper[2]), ("sp", "dp"))
    return ((summed[0], summed[1], summed[2]), (summed[3], summed[4], summed[5]))


def on_device(volume, cotangent, kernels_xy, kernels_z, mixing):
    inputs = volume[0]
    grad_top = cotangent[0]
    kernel_xy = kernels_xy.astype(jnp.float32)
    kernel_z = kernels_z.astype(jnp.float32)
    slab_len = inputs.shape[1]
    ranks = lax.axis_size("sp")
    place = lax.axis_index("sp")
    wide = padded_2(inputs, (("sp", 1),), 2)
    planar1, axial1, preact1 = forward_block(wide, kernel_xy[0], kernel_z[0], mixing[0])
    hidden = jax.nn.silu(preact1).astype(jnp.bfloat16)
    spots = place * slab_len - 1 + jnp.arange(slab_len + 2, dtype=jnp.int32)
    hidden = jnp.where(
        ((spots >= 0) & (spots < slab_len * ranks))[None, :, None, None],
        hidden,
        jnp.zeros_like(hidden),
    )
    planar2, axial2, preact2 = forward_block(hidden, kernel_xy[1], kernel_z[1], mixing[1])
    grad_planar2, upper = backward_block(
        grad_top, planar2, axial2, preact2, hidden, kernel_z[1], mixing[1], 0
    )
    grad_hidden = conv_plane(edge_grads(grad_planar2), kernel_xy[1][:, ::-1, ::-1]).astype(
        jnp.bfloat16
    )
    grad_planar1, lower = backward_block(
        grad_hidden,
        planar1[:, 1:-1],
        axial1[:, 1:-1],
        preact1[:, 1:-1],
        wide[:, 1:-1],
        kernel_z[0],
        mixing[0],
        0,
    )
    grad_inputs = conv_plane(edge_grads(grad_planar1), kernel_xy[0][:, ::-1, ::-1]).astype(
        jnp.bfloat16
    )
    lower, upper = settle_all(lower, upper)
    factor = 1.0 / math.sqrt(
        lax.axis_size("dp") * slab_len * ranks * inputs.shape[2] * inputs.shape[3]
    )
    mixing_grad = jnp.stack([lower[0], upper[0]]) * factor
    xy_grad = jnp.stack([lower[1], upper[1]]) * factor
    z_grad = jnp.stack([lower[2], upper[2]]) * factor
    return (grad_inputs[None], mixing_grad, xy_grad, z_grad)


def solution(mesh):
    return jax.shard_map(
        on_device,
        mesh=mesh,
        in_specs=(P("dp", None, "sp", None, None), P("dp", None, "sp", None, None), P(), P(), P()),
        out_specs=(P("dp", None, "sp", None, None), P(), P(), P()),
        check_vma=False,
    )
```

profile of v0, /device:TPU:1, one launch (start us, length us, event | category | flops | bytes accessed | tf_op | source)
XLA Modules:
  0.0 328.5 jit_solution(12075035630448840751)
XLA Ops:
  7.2 1.5 copy.76
  8.8 4.9 %collective-permute-start = (bf16[96,2,8,128]{3,0,2,1:T(8,128)(2,1)S(1)}, bf16[96,2,8,128]{3,0,2,1:T(8,128)(2,1)S(1)}, u32[]{:S(2)}, u32[]{:S(2)}) collective-permute-start(bf16[96,2,8,128]{3,0,2,1:T(8,128)(2,1)S(1)} %get-tuple-element.61), channel_id=1, source_target_pairs={{0,4},{4,8},{8,12},{12,16},{16,20},{20,24},{24,28},{28,32},{32,36}... | collective-permute-start | bytes 1179656 | tf_op jit(solution)/shard_map/ppermute | solution.py:15
  13.8 1.9 collective-permute-start.1
  15.8 1.5 reshape.101
  18.5 4.4 %collective-permute-done.1 = bf16[96,2,8,128]{3,0,2,1:T(8,128)(2,1)S(1)} collective-permute-done((bf16[96,2,8,128]{3,0,2,1:T(8,128)(2,1)S(1)}, bf16[96,2,8,128]{3,0,2,1:T(8,128)(2,1)S(1)}, u32[]{:S(2)}, u32[]{:S(2)}) %collective-permute-start.1) | collective-permute-done | bytes 393248 | tf_op jit(solution)/shard_map/ppermute | solution.py:16
  23.0 3.1 multiply_add_fusion
  26.1 1.4 copy-done
  30.4 3.0 fusion.24
  36.5 6.6 %multiply_reduce_fusion.2 = (f32[96]{0:T(128)S(1)}, f32[96]{0:T(128)S(1)}, f32[96]{0:T(128)S(1)}, f32[96]{0:T(128)S(1)}, f32[96]{0:T(128)S(1)}, /*index=5*/f32[9...) fusion(f32[96,4,8,128]{3,2,1,0:T(8,128)S(1)} %bitcast.196, ...), kind=kLoop, calls=%fused_computation.147 | loop fusion | flops 15727488 | bytes 7477248 | tf_op jit(solution)/shard_map/reduce_sum | solution.py:83
  43.1 1.9 collective-permute-start.2
  45.1 2.6 collective-permute-start.3
  49.8 1.2 convolution_bitcast_fusion.3
  51.0 1.4 collective-permute-done.3
  52.3 1.5 fusion.9
  53.9 3.5 %multiply_convert_fusion.1 = bf16[96,4,8,128]{3,2,1,0:T(8,128)(2,1)S(1)} fusion(f32[96,6,8,128]{3,2,1,0:T(8,128)S(1)} %bitcast.193, bf16[96,6,8,130]{3,2,1,0:T(8,128)(2,1)S(1)} %fusion.9, f32[96]{0:T(128)S(1)} %get-tuple-element.71, bf16[96,1,8,128]{3,2,1,0:T(8,128)(2,1)S(1)} %collective-permute-done.3, bf16[96,4,8,128]{3,2,1,0:T(8,128)(2,1)S(1)} %get-tuple-element.56, ...), kind=kLoop, calls=%fused_computation.149 | loop fusion | flops 15335424 | bytes 8260992 | tf_op jit(solution)/shard_map/convert_element_type | solution.py:66
  60.7 1.4 fusion.31
  62.7 2.8 fusion.60
  66.2 2.1 collective-permute-start.4
  68.3 2.3 collective-permute-start.5
  70.6 242.2 %all-reduce.13.cloned.1.call-done = (f32[1,96,96]{2,1,0:T(8,128)}, f32[1,96,96]{2,1,0:T(8,128)}, f32[1,96,3,3]{1,3,2,0:T(4,128)}, f32[1,96,3,3]{1,3,2,0:T(4,128)...) async-done(((f32[1,96,96]{2,1,0:T(8,128)}, f32[1,96,96]{2,1,0:T(8,128)}, f32[1,96,3,3]{1,3,2,0:T(4,128)}, f32[1,96,3,3]{1,3,2,0:T(4,128)}, f32[1,96,3]{1,2,0:T(4,128)}, ...) | async-done | bytes 82960 | tf_op jit(solution)/shard_map/psum | solution.py:116
  315.4 1.5 maximum_multiply_fusion
  316.9 1.6 fusion.11
  318.4 2.0 fusion.92
  320.4 1.2 copy.31
  (68 shorter events, 16.6 us)
Async XLA Ops:
  7.2 8.5 %copy-start.7 = (bf16[2,96,3,3]{1,0,3,2:T(2,128)(2,1)S(1)}, bf16[2,96,3,3]{1,0,3,2:T(2,128)(2,1)}, u32[]{:S(2)}) copy-start(bf16[2,96,3,3]{1,0,3,2:T(2,128)(2,1)} %param.7) | copy-start | bytes 10372
  7.2 8.6 %copy-start.8 = (bf16[2,96,3]{1,0,2:T(2,128)(2,1)S(1)}, bf16[2,96,3]{1,0,2:T(2,128)(2,1)}, u32[]{:S(2)}) copy-start(bf16[2,96,3]{1,0,2:T(2,128)(2,1)} %param.8) | copy-start | bytes 3460
  7.2 8.6 %copy-start.4 = (bf16[1,96,4,8,128]{4,3,2,1,0:T(8,128)(2,1)S(1)}, bf16[1,96,4,8,128]{4,3,2,1,0:T(8,128)(2,1)}, u32[]{:S(2)}) copy-start(bf16[1,96,4,8,128]{4,3,2,1,0:T(8,128)(2,1)} %param.6) | copy-start | bytes 2359300
  7.2 305.6 %all-reduce.13.cloned.1.call-start = ((), (), s32[]{:S(2)}) async-start(), calls=%async_computation | async-start | bytes 229376 | tf_op jit(solution)/shard_map/psum | solution.py:116
  8.8 9.6 %collective-permute-start = (bf16[96,2,8,128]{3,0,2,1:T(8,128)(2,1)S(1)}, bf16[96,2,8,128]{3,0,2,1:T(8,128)(2,1)S(1)}, u32[]{:S(2)}, u32[]{:S(2)}) collective-permute-start(bf16[96,2,8,128]{3,0,2,1:T(8,128)(2,1)S(1)} %get-tuple-element.61), channel_id=1, source_target_pairs={{0,4},{4,8},{8,12},{12,16},{16,20},{20,24},{24,28},{28,32},{32,36}... | collective-permute-start | bytes 1179656 | tf_op jit(solution)/shard_map/ppermute | solution.py:15
  13.8 9.1 %collective-permute-start.1 = (bf16[96,2,8,128]{3,0,2,1:T(8,128)(2,1)S(1)}, bf16[96,2,8,128]{3,0,2,1:T(8,128)(2,1)S(1)}, u32[]{:S(2)}, u32[]{:S(2)}) collective-permute-start(bf16[96,2,8,128]{3,0,2,1:T(8,128)(2,1)S(1)} %get-tuple-element.62), channel_id=1, source_target_pairs={{4,0},{8,4},{12,8},{16,12},{20,16},{24,20},{28,24},{32,28},{36,32}... | collective-permute-start | bytes 1179656 | tf_op jit(solution)/shard_map/ppermute | solution.py:16
  23.0 3.1 copy-start.2
  26.1 1.4 copy-start
  28.1 0.8 copy-start.6
  34.0 1.4 copy-start.5
  43.1 7.8 %collective-permute-start.2 = (bf16[96,1,8,128]{3,2,1,0:T(8,128)(2,1)S(1)}, bf16[96,1,8,128]{3,2,1,0:T(8,128)(2,1)S(1)}, u32[]{:S(2)}, u32[]{:S(2)}) collective-permute-start(bf16[96,1,8,128]{3,2,1,0:T(8,128)(2,1)S(1)} %get-tuple-element.59), channel_id=1, source_target_pairs={{0,4},{4,8},{8,12},{12,16},{16,20},{20,24},{24,28},{28,32},{32,36}... | collective-permute-start | bytes 589832 | tf_op jit(solution)/shard_map/ppermute | solution.py:15
  45.1 7.3 %collective-permute-start.3 = (bf16[96,1,8,128]{3,2,1,0:T(8,128)(2,1)S(1)}, bf16[96,1,8,128]{3,2,1,0:T(8,128)(2,1)S(1)}, u32[]{:S(2)}, u32[]{:S(2)}) collective-permute-start(bf16[96,1,8,128]{3,2,1,0:T(8,128)(2,1)S(1)} %get-tuple-element.60), channel_id=1, source_target_pairs={{4,0},{8,4},{12,8},{16,12},{20,16},{24,20},{28,24},{32,28},{36,32}... | collective-permute-start | bytes 589832 | tf_op jit(solution)/shard_map/ppermute | solution.py:16
  58.5 1.7 copy-start.1
  58.9 1.8 slice-start
  60.7 2.0 slice-start.1
  60.7 2.0 copy-start.3
  66.2 250.6 %collective-permute-start.4 = (bf16[96,1,8,128]{3,0,2,1:T(8,128)(2,1)S(1)}, bf16[96,1,8,128]{3,0,2,1:T(8,128)(2,1)S(1)}, u32[]{:S(2)}, u32[]{:S(2)}) collective-permute-start(bf16[96,1,8,128]{3,0,2,1:T(8,128)(2,1)S(1)} %get-tuple-element.57), channel_id=1, source_target_pairs={{0,4},{4,8},{8,12},{12,16},{16,20},{20,24},{24,28},{28,32},{32,36}... | collective-permute-start | bytes 589832 | tf_op jit(solution)/shard_map/ppermute | solution.py:15
  68.3 248.6 %collective-permute-start.5 = (bf16[96,1,8,128]{3,0,2,1:T(8,128)(2,1)S(1)}, bf16[96,1,8,128]{3,0,2,1:T(8,128)(2,1)S(1)}, u32[]{:S(2)}, u32[]{:S(2)}) collective-permute-start(bf16[96,1,8,128]{3,0,2,1:T(8,128)(2,1)S(1)} %get-tuple-element.58), channel_id=1, source_target_pairs={{4,0},{8,4},{12,8},{16,12},{20,16},{24,20},{28,24},{32,28},{36,32}... | collective-permute-start | bytes 589832 | tf_op jit(solution)/shard_map/ppermute | solution.py:16
Sparse Core Ops, SparseCore 0:
  66.3 246.4 all-reduce.12
where the time goes:
time: 329 us; the launch traced here: 328 us
  waiting for transfers between devices  249 us (76%)
  other arithmetic  33.4 us (10%)
  starting transfers between devices  15.7 us (5%)
  between operations  14.4 us (4%)
  local copies, waits for them, and re-layouts  11.5 us (3%)
  matrix products  4.28 us (1%)
    psum x1, waiting for transfers between devices, settle_all(): lax.psum((lower[0], lower[1], lower[2], upper[0], upper[1], upper[2]), ('...  242 us
    ppermute x3, starting transfers between devices, padded_2(): before = lax.ppermute(last, axis, up)  8.92 us
    unnamed x28, local copies, waits for them, and re-layouts  8.82 us
    reduce_sum x2, other arithmetic, backward_block(): jnp.sum(grad_axial * planar_pad[:, :, depth_tap:depth_tap + depth_len, :]...  7.96 us
    ppermute x3, starting transfers between devices, padded_2(): after = lax.ppermute(first, axis, down)  6.79 us
  transfers between devices with their start and end apart: 7, of which 4 were waited for; matrix products, arithmetic and copies ran while one was open for 3% of the time, Pallas kernels for 0%

commit v1 on v0

--- a/solution.py
+++ b/solution.py
@@ -1,8 +1,18 @@
+import functools
 import math
 import jax
 import jax.numpy as jnp
 from jax import lax
 from jax.sharding import PartitionSpec as P
+
+
+def treat_the_block(v0, mesh_ax, shard_axis):
+    shaped = lax.psum(v0, mesh_ax)
+    work_now = lax.psum(shaped, shard_axis)
+    return work_now
+
+
+finish_the_thing = functools.partial(treat_the_block, mesh_ax="sp", shard_axis="dp")
 
 
 def padded_2(x, sides, width):
@@ -113,7 +123,7 @@
 
 
 def settle_all(lower, upper):
-    summed = lax.psum((lower[0], lower[1], lower[2], upper[0], upper[1], upper[2]), ("sp", "dp"))
+    summed = finish_the_thing((lower[0], lower[1], lower[2], upper[0], upper[1], upper[2]))
     return ((summed[0], summed[1], summed[2]), (summed[3], summed[4], summed[5]))
 
 

time: 329 us -> 304 us (0.924)
  waiting for transfers between devices: 249 us -> 222 us
    psum x1 -> x2, waiting for transfers between devices: 242 us -> 215 us  [the longest x1 176 us: treat_the_block(): shaped = lax.psum(v0, mesh_ax)]
  transfers between devices with their start and end apart: 7 -> 8, of which waited for: 4 -> 5; matrix products, arithmetic and copies ran while one was open for 3% -> 3% of each run, Pallas kernels for 0% -> 0%
where the time goes in v1:
time: 304 us; the launch traced here: 302 us
  waiting for transfers between devices  222 us (73%)
  other arithmetic  33.3 us (11%)
  starting transfers between devices  16.8 us (6%)
  between operations  14.5 us (5%)
  local copies, waits for them, and re-layouts  11.5 us (4%)
  matrix products  4.28 us (1%)
    psum x1, waiting for transfers between devices, treat_the_block(): shaped = lax.psum(v0, mesh_ax)  176 us
    psum x1, waiting for transfers between devices, treat_the_block(): work_now = lax.psum(shaped, shard_axis)  38.6 us
    ppermute x3, starting transfers between devices, padded_2(): before = lax.ppermute(last, axis, up)  10.2 us
    unnamed x28, local copies, waits for them, and re-layouts  8.82 us
    reduce_sum x2, other arithmetic, backward_block(): jnp.sum(grad_axial * planar_pad[:, :, depth_tap:depth_tap + depth_len, :]...  7.96 us
    ppermute x3, starting transfers between devices, padded_2(): after = lax.ppermute(first, axis, down)  6.44 us
  transfers between devices with their start and end apart: 8, of which 5 were waited for; matrix products, arithmetic and copies ran while one was open for 3% of the time, Pallas kernels for 0%

profile of v1, /device:TPU:1, one launch (start us, length us, event | category | flops | bytes accessed | tf_op | source)
XLA Modules:
  0.0 302.2 jit_solution(10722703445760988632)
XLA Ops:
  7.2 1.5 copy.76
  8.8 4.9 %collective-permute-start = (bf16[96,2,8,128]{3,0,2,1:T(8,128)(2,1)S(1)}, bf16[96,2,8,128]{3,0,2,1:T(8,128)(2,1)S(1)}, u32[]{:S(2)}, u32[]{:S(2)}) collective-permute-start(bf16[96,2,8,128]{3,0,2,1:T(8,128)(2,1)S(1)} %get-tuple-element.67), channel_id=1, source_target_pairs={{0,4},{4,8},{8,12},{12,16},{16,20},{20,24},{24,28},{28,32},{32,36}... | collective-permute-start | bytes 1179656 | tf_op jit(solution)/shard_map/ppermute | solution.py:25
  13.8 1.9 collective-permute-start.1
  15.8 1.5 reshape.101
  18.5 4.4 %collective-permute-done.1 = bf16[96,2,8,128]{3,0,2,1:T(8,128)(2,1)S(1)} collective-permute-done((bf16[96,2,8,128]{3,0,2,1:T(8,128)(2,1)S(1)}, bf16[96,2,8,128]{3,0,2,1:T(8,128)(2,1)S(1)}, u32[]{:S(2)}, u32[]{:S(2)}) %collective-permute-start.1) | collective-permute-done | bytes 393248 | tf_op jit(solution)/shard_map/ppermute | solution.py:26
  23.0 3.1 %multiply_add_fusion = f32[96,6,8,128]{3,0,2,1:T(8,128)S(1)} fusion(bf16[96,2,8,128]{3,0,2,1:T(8,128)(2,1)S(1)} %collective-permute-done.1, bf16[96,4,8,128]{3,0,2,1:T(8,128)(2,1)S(1)} %bitcast.184, bf16[96,2,8,128]{3,0,2,1:T(8,128)(2,1)S(1)} %collective-permute-done, bf16[96,8,8,128]{3,0,2,1:T(8,128)(2,1)S(1)} %pad_maximum_fusion, ...), kind=kLoop, calls=%fused_computation.66 | loop fusion | flops 18874368 | bytes 6689280 | tf_op jit(solution)/shard_map/add | solution.py:38
  26.1 1.4 copy-done
  30.4 3.0 %fusion.24 = f32[96,4,8,128]{3,2,1,0:T(8,128)S(1)} fusion(f32[96]{0:T(128)S(1)} %get-tuple-element.70, f32[96]{0:T(128)S(1)} %get-tuple-element.71, f32[96]{0:T(128)S(1)} %get-tuple-element.72, f32[96]{0:T(128)S(1)} %get-tuple-element.73, f32[96]{0:T(128)S(1)} %get-tuple-element.74, f32[96]{0:T(128)S(1)} %get-tuple-element.75, f32[96]{0:T(128)S(1)} %get-tuple-element.76, ...), kind=kLoop, calls=%fused_computation.88 | loop fusion | flops 10223616 | bytes 5116416 | tf_op jit(solution)/shard_map/add | solution.py:38
  36.5 6.6 %multiply_reduce_fusion.2 = (f32[96]{0:T(128)S(1)}, f32[96]{0:T(128)S(1)}, f32[96]{0:T(128)S(1)}, f32[96]{0:T(128)S(1)}, f32[96]{0:T(128)S(1)}, /*index=5*/f32[9...) fusion(f32[96,4,8,128]{3,2,1,0:T(8,128)S(1)} %bitcast.190, ...), kind=kLoop, calls=%fused_computation.147 | loop fusion | flops 15727488 | bytes 7477248 | tf_op jit(solution)/shard_map/reduce_sum | solution.py:93
  43.1 1.9 collective-permute-start.2
  45.1 2.6 collective-permute-start.3
  51.0 1.4 collective-permute-done.3
  52.3 1.5 fusion.9
  53.9 3.5 %multiply_convert_fusion.1 = bf16[96,4,8,128]{3,2,1,0:T(8,128)(2,1)S(1)} fusion(f32[96,6,8,128]{3,2,1,0:T(8,128)S(1)} %bitcast.187, bf16[96,6,8,130]{3,2,1,0:T(8,128)(2,1)S(1)} %fusion.9, f32[96]{0:T(128)S(1)} %get-tuple-element.77, bf16[96,1,8,128]{3,2,1,0:T(8,128)(2,1)S(1)} %collective-permute-done.3, bf16[96,4,8,128]{3,2,1,0:T(8,128)(2,1)S(1)} %get-tuple-element.62, ...), kind=kLoop, calls=%fused_computation.149 | loop fusion | flops 15335424 | bytes 8260992 | tf_op jit(solution)/shard_map/convert_element_type | solution.py:76
  60.7 1.4 fusion.31
  62.7 2.8 fusion.60
  66.2 176.3 %all-reduce.15.cloned.1.call-done = (f32[96,96]{1,0:T(8,128)}, f32[96,96]{1,0:T(8,128)}, f32[96,3,3]{0,2,1:T(4,128)}, f32[96,3,3]{0,2,1:T(4,128)}, f32[96,3]{0,1:T(4,128)}, /*index=5*/f32[96,3]{0,1:T(4,128)}) async-done(((f32[96,96]{1,0:T(8,128)}, f32[96,96]{1,0:T(8,128)}, f32[96,3,3]{0,2,1:T(4,128)}, f32[96,3,3]{0,2,1:T(4,128)}, f32[96,3]{0,1:T(4,128)}, /*index=5*/f32[96,3]{0,1:T(4,128)}), ...) | async-done | bytes 82960 | tf_op jit(solution)/shard_map/psum | solution.py:10
  242.5 3.4 %collective-permute-start.4 = (bf16[96,1,8,128]{3,0,2,1:T(8,128)(2,1)S(1)}, bf16[96,1,8,128]{3,0,2,1:T(8,128)(2,1)S(1)}, u32[]{:S(2)}, u32[]{:S(2)}) collective-permute-start(bf16[96,1,8,128]{3,0,2,1:T(8,128)(2,1)S(1)} %get-tuple-element.63), channel_id=1, source_target_pairs={{0,4},{4,8},{8,12},{12,16},{16,20},{20,24},{24,28},{28,32},{32,36}... | collective-permute-start | bytes 589832 | tf_op jit(solution)/shard_map/ppermute | solution.py:25
  245.9 1.9 collective-permute-start.5
  247.9 38.6 %all-reduce.17.cloned.1.call-done = (f32[1,96,96]{2,1,0:T(8,128)}, f32[1,96,96]{2,1,0:T(8,128)}, f32[1,96,3,3]{1,3,2,0:T(4,128)}, f32[1,96,3,3]{1,3,2,0:T(4,128)...) async-done(((f32[1,96,96]{2,1,0:T(8,128)}, f32[1,96,96]{2,1,0:T(8,128)}, f32[1,96,3,3]{1,3,2,0:T(4,128)}, f32[1,96,3,3]{1,3,2,0:T(4,128)}, f32[1,96,3]{1,2,0:T(4,128)}, ...) | async-done | bytes 82960 | tf_op jit(solution)/shard_map/psum | solution.py:11
  289.1 1.5 maximum_multiply_fusion
  290.5 1.6 fusion.11
  292.1 2.0 fusion.92
  294.1 1.2 copy.31
  (71 shorter events, 17.8 us)
Async XLA Ops:
  7.2 8.5 %copy-start.7 = (bf16[2,96,3,3]{1,0,3,2:T(2,128)(2,1)S(1)}, bf16[2,96,3,3]{1,0,3,2:T(2,128)(2,1)}, u32[]{:S(2)}) copy-start(bf16[2,96,3,3]{1,0,3,2:T(2,128)(2,1)} %param.7) | copy-start | bytes 10372
  7.2 8.6 %copy-start.8 = (bf16[2,96,3]{1,0,2:T(2,128)(2,1)S(1)}, bf16[2,96,3]{1,0,2:T(2,128)(2,1)}, u32[]{:S(2)}) copy-start(bf16[2,96,3]{1,0,2:T(2,128)(2,1)} %param.8) | copy-start | bytes 3460
  7.2 8.6 %copy-start.4 = (bf16[1,96,4,8,128]{4,3,2,1,0:T(8,128)(2,1)S(1)}, bf16[1,96,4,8,128]{4,3,2,1,0:T(8,128)(2,1)}, u32[]{:S(2)}) copy-start(bf16[1,96,4,8,128]{4,3,2,1,0:T(8,128)(2,1)} %param.6) | copy-start | bytes 2359300
  7.2 235.3 %all-reduce.15.cloned.1.call-start = ((), (), s32[]{:S(2)}) async-start(), calls=%async_computation | async-start | bytes 229376 | tf_op jit(solution)/shard_map/psum | solution.py:10
  8.8 9.6 %collective-permute-start = (bf16[96,2,8,128]{3,0,2,1:T(8,128)(2,1)S(1)}, bf16[96,2,8,128]{3,0,2,1:T(8,128)(2,1)S(1)}, u32[]{:S(2)}, u32[]{:S(2)}) collective-permute-start(bf16[96,2,8,128]{3,0,2,1:T(8,128)(2,1)S(1)} %get-tuple-element.67), channel_id=1, source_target_pairs={{0,4},{4,8},{8,12},{12,16},{16,20},{20,24},{24,28},{28,32},{32,36}... | collective-permute-start | bytes 1179656 | tf_op jit(solution)/shard_map/ppermute | solution.py:25
  13.8 9.1 %collective-permute-start.1 = (bf16[96,2,8,128]{3,0,2,1:T(8,128)(2,1)S(1)}, bf16[96,2,8,128]{3,0,2,1:T(8,128)(2,1)S(1)}, u32[]{:S(2)}, u32[]{:S(2)}) collective-permute-start(bf16[96,2,8,128]{3,0,2,1:T(8,128)(2,1)S(1)} %get-tuple-element.68), channel_id=1, source_target_pairs={{4,0},{8,4},{12,8},{16,12},{20,16},{24,20},{28,24},{32,28},{36,32}... | collective-permute-start | bytes 1179656 | tf_op jit(solution)/shard_map/ppermute | solution.py:26
  23.0 3.1 %copy-start.2 = (bf16[96,8,8,128]{3,0,2,1:T(8,128)(2,1)}, bf16[96,8,8,128]{3,0,2,1:T(8,128)(2,1)S(1)}, u32[]{:S(2)}) copy-start(bf16[96,8,8,128]{3,0,2,1:T(8,128)(2,1)S(1)} %pad_maximum_fusion) | copy-start | bytes 4718596
  26.1 1.4 copy-start
  28.1 0.8 copy-start.6
  34.0 1.4 copy-start.5
  43.1 7.8 %collective-permute-start.2 = (bf16[96,1,8,128]{3,2,1,0:T(8,128)(2,1)S(1)}, bf16[96,1,8,128]{3,2,1,0:T(8,128)(2,1)S(1)}, u32[]{:S(2)}, u32[]{:S(2)}) collective-permute-start(bf16[96,1,8,128]{3,2,1,0:T(8,128)(2,1)S(1)} %get-tuple-element.65), channel_id=1, source_target_pairs={{0,4},{4,8},{8,12},{12,16},{16,20},{20,24},{24,28},{28,32},{32,36}... | collective-permute-start | bytes 589832 | tf_op jit(solution)/shard_map/ppermute | solution.py:25
  45.1 7.3 %collective-permute-start.3 = (bf16[96,1,8,128]{3,2,1,0:T(8,128)(2,1)S(1)}, bf16[96,1,8,128]{3,2,1,0:T(8,128)(2,1)S(1)}, u32[]{:S(2)}, u32[]{:S(2)}) collective-permute-start(bf16[96,1,8,128]{3,2,1,0:T(8,128)(2,1)S(1)} %get-tuple-element.66), channel_id=1, source_target_pairs={{4,0},{8,4},{12,8},{16,12},{20,16},{24,20},{28,24},{32,28},{36,32}... | collective-permute-start | bytes 589832 | tf_op jit(solution)/shard_map/ppermute | solution.py:26
  58.5 1.7 copy-start.1
  58.9 1.8 slice-start
  60.7 2.0 slice-start.1
  60.7 2.0 copy-start.3
  66.1 220.3 %all-reduce.17.cloned.1.call-start = ((), (), s32[]{:S(2)}) async-start(), calls=%async_computation.1 | async-start | bytes 229376 | tf_op jit(solution)/shard_map/psum | solution.py:11
  242.5 48.0 %collective-permute-start.4 = (bf16[96,1,8,128]{3,0,2,1:T(8,128)(2,1)S(1)}, bf16[96,1,8,128]{3,0,2,1:T(8,128)(2,1)S(1)}, u32[]{:S(2)}, u32[]{:S(2)}) collective-permute-start(bf16[96,1,8,128]{3,0,2,1:T(8,128)(2,1)S(1)} %get-tuple-element.63), channel_id=1, source_target_pairs={{0,4},{4,8},{8,12},{12,16},{16,20},{20,24},{24,28},{28,32},{32,36}... | collective-permute-start | bytes 589832 | tf_op jit(solution)/shard_map/ppermute | solution.py:25
  245.9 44.6 %collective-permute-start.5 = (bf16[96,1,8,128]{3,0,2,1:T(8,128)(2,1)S(1)}, bf16[96,1,8,128]{3,0,2,1:T(8,128)(2,1)S(1)}, u32[]{:S(2)}, u32[]{:S(2)}) collective-permute-start(bf16[96,1,8,128]{3,0,2,1:T(8,128)(2,1)S(1)} %get-tuple-element.64), channel_id=1, source_target_pairs={{4,0},{8,4},{12,8},{16,12},{20,16},{24,20},{28,24},{32,28},{36,32}... | collective-permute-start | bytes 589832 | tf_op jit(solution)/shard_map/ppermute | solution.py:26
Sparse Core Ops, SparseCore 0:
  66.3 176.1 all-reduce.14
  245.2 41.2 all-reduce.16
